TPU v7x, 512 devices: a whole 4x4x16 slice. The times are simulated.
512 devices in a mesh: dp: 8 (over y, core), expert: 64 (over x, z).
Axes of the slice: x: 4, y: 4, z: 16, core: 2. Of those that a mesh axis runs over, the one named last changes fastest.
Arguments:
- grad_out: bfloat16 [32768, 4096], P('expert', 'dp'), may hold values from -30 to 30
- hidden: bfloat16 [32768, 2, 1024], P('expert', None, 'dp'), may hold values from -24 to 24
- gate_prob: float32 [32768, 2], P('expert'), may hold values from 0.05 to 1
- expert_ids: int32 [32768, 2], P('expert'), may hold values from 0 to 63, all different within a row; in each aligned block of 512 rows (0 to 511, 512 to 1023, ...) at most 20 rows name the same one
- weights: bfloat16 [64, 1024, 4096], P('expert', None, 'dp'), may hold values from -0.1875 to 0.1875
Outputs:
- hidden_grad: bfloat16 [32768, 2, 1024], P('expert', None, 'dp')
- update: float32 [64, 1024, 4096], P('expert', None, 'dp')
Inputs may be any that keep to these rules, and one draw needn't show every extreme that they name: `expert_ids`: among the 512 tokens of one index of expert, no expert is named by more than 20 choices, a bound that some block reaches; the 2 experts of a token differ.
All inputs are finite; a program needn't handle non-finite values.
Results may differ from a plain program's by a relative error of at most 0.019.
Values may be sent and summed in bfloat16 or wider, within the bound.
No kernel may reach another device: no remote copies, remote signals or barrier semaphores. Data moves between devices by JAX's collectives and lax.ppermute only.
A program may use at most 64 MiB of HBM per device.

v0:
```python
import jax
import jax.numpy as jnp
from jax import lax
from jax.sharding import PartitionSpec as P

D = 4096


def slot_numbers(route_ids, capacity, expert_count):
    flat_ids = route_ids.reshape(-1)
    one_hot = (flat_ids[:, None] == jnp.arange(expert_count, dtype=jnp.int32)[None, :]).astype(
        jnp.int32
    )
    before = jnp.cumsum(one_hot, axis=0) - one_hot
    rank_in = jnp.sum(before * one_hot, axis=1)
    return flat_ids * capacity + rank_in


def gram_sum(matrix_part):
    partial_gram = jnp.dot(matrix_part, matrix_part.T, preferred_element_type=jnp.float32)
    return lax.psum(partial_gram.astype(jnp.bfloat16), "dp").astype(jnp.float32)


def place_slots(slot_index, values, slot_count):
    empty_rows = jnp.zeros((slot_count,) + values.shape[1:], values.dtype)
    return empty_rows.at[slot_index].set(values)


def per_device(grad_out, hidden, gate_prob, expert_ids, weights):
    tokens, width_part = grad_out.shape
    top_count = expert_ids.shape[1]
    experts = lax.axis_size("expert")
    capacity = 5 * tokens * top_count // (4 * experts)
    total_slots = experts * capacity
    pair_count = tokens * top_count
    slot_index = slot_numbers(expert_ids, capacity, experts)
    token_of = jnp.arange(pair_count, dtype=jnp.int32) // top_count
    send_grad = place_slots(slot_index, grad_out[token_of], total_slots).reshape(
        experts, capacity, width_part
    )
    scaled_part = (gate_prob[:, :, None] * hidden.astype(jnp.float32)).astype(jnp.bfloat16)
    whole_scaled = lax.all_gather(scaled_part, "dp", axis=2, tiled=True)
    send_scaled = place_slots(
        slot_index, whole_scaled.reshape(pair_count, -1), total_slots
    ).reshape(experts, capacity, -1)
    got_grad, got_scaled = (
        lax.all_to_all(send_grad, "expert", split_axis=0, concat_axis=0, tiled=True),
        lax.all_to_all(send_scaled, "expert", split_axis=0, concat_axis=0, tiled=True),
    )
    got_grad = got_grad.reshape(total_slots, width_part)
    got_scaled = got_scaled.reshape(total_slots, -1)
    weight_part = weights[0]
    gradient = lax.dot_general(
        got_scaled, got_grad, (((0,), (0,)), ((), ())), preferred_element_type=jnp.float32
    )
    back_term = lax.dot_general(
        got_grad, weight_part, (((1,), (1,)), ((), ())), preferred_element_type=jnp.float32
    )
    flat_prob = gate_prob.reshape(-1)
    summed = lax.psum_scatter(
        back_term.astype(jnp.bfloat16), "dp", scatter_dimension=1, tiled=True
    ).astype(jnp.float32)
    returned = lax.all_to_all(
        summed.reshape(experts, capacity, -1).astype(jnp.bfloat16),
        "expert",
        split_axis=0,
        concat_axis=0,
        tiled=True,
    ).astype(jnp.float32)
    picked = returned.reshape(total_slots, -1)[slot_index]
    hidden_grad = (flat_prob[:, None] * picked).astype(jnp.bfloat16).reshape(tokens, top_count, -1)
    grad_bf16 = gradient.astype(jnp.bfloat16)
    gram_first = gram_sum(grad_bf16)
    norm_sq = jnp.sqrt(jnp.sum(gram_first * gram_first)) + 1e-06
    current = (grad_bf16.astype(jnp.float32) * lax.rsqrt(norm_sq)).astype(jnp.bfloat16)
    gram_now = (gram_first / norm_sq).astype(jnp.bfloat16)
    following = current.astype(jnp.float32)
    for sweep_number in range(2):
        if sweep_number > 0:
            gram_now = gram_sum(current).astype(jnp.bfloat16)
        following = 1.5 * current.astype(jnp.float32) - 0.5 * jnp.dot(
            gram_now, current, preferred_element_type=jnp.float32
        )
        current = following.astype(jnp.bfloat16)
    update = following * D**0.5
    return (hidden_grad, update[None])


def solution(mesh):
    in_specs = (
        P("expert", "dp"),
        P("expert", None, "dp"),
        P("expert", None),
        P("expert", None),
        P("expert", None, "dp"),
    )
    out_specs = (P("expert", None, "dp"), P("expert", None, "dp"))
    return jax.shard_map(
        per_device, mesh=mesh, in_specs=in_specs, out_specs=out_specs, check_vma=False
    )
```

profile of v0, /device:TPU:2, one launch (start us, length us, event | category | flops | bytes accessed | tf_op | source)
XLA Modules:
  0.0 626.0 jit_solution(6197987789082699378)
XLA Ops:
  7.2 0.0 copy-start
  7.2 0.0 reduce-scatter.4.cloned.1.call-start
  7.2 0.8 broadcast_multiply_fusion
  8.0 0.8 copy.19
  8.8 0.2 eq.29
  9.0 0.2 eq.25
  9.2 0.1 copy.18
  9.3 0.2 mul.64
  9.6 18.0 %reduce-window.6 = s32[64,8,128]{2,1,0:T(8,128)S(1)} reduce-window(s32[64,8,128]{2,1,0:T(8,128)S(1)} %fusion.21, s32[]{:T(128)} %constant.16.clone.1), window={size=1x1x128 pad=0_0x0_0x127_0}, to_apply=%region_0.0 | reduce-window | flops 8323072 | bytes 524292 | tf_op jit(solution)/shard_map/reduce-window
  27.6 0.1 slice.12
  27.7 0.1 copy.21
  27.9 0.1 copy.22
  28.0 0.1 broadcast_add_fusion
  28.1 0.1 fusion.20
  28.2 12.8 %scatter_custom_fusion = bf16[1280,512]{1,0:T(8,128)(2,1)S(1)} fusion(s32[1024]{0:T(1024)S(1)} %bitcast.46, bf16[512,512]{1,0:T(8,128)(2,1)} %param.5, s32[1024]{0:T(1024)S(1)} %broadcast_clamp_fusion.1, bf16[]{:T(256)} %constant.13.clone.1), kind=kCustom, calls=%fused_computation.22 | custom fusion | bytes 1311232 | tf_op jit(solution)/shard_map/scatter | solution.py:26
  41.0 1.3 reshape.124
  42.3 94.8 %all_to_all.15 = bf16[64,20,512]{2,1,0:T(8,128)(2,1)S(1)} all-to-all(bf16[64,20,512]{2,1,0:T(8,128)(2,1)} %reshape.124), channel_id=1, replica_groups=mesh['dp'=8,'expert'=64] {'expert'}, dimensions={0} | all-to-all | bytes 2621440 | tf_op jit(solution)/shard_map/all_to_all | solution.py:47
  137.1 1.2 reshape.125
  138.3 0.0 copy-done
  138.3 4.4 convolution_convert_fusion
  142.7 4.4 copy.25
  147.1 0.0 copy-start.2
  147.1 0.0 reduce-scatter.4.cloned.1.call-update
  147.1 35.3 %reduce-scatter.4.cloned.1.call-done = bf16[128,1280]{1,0:T(8,128)(2,1)} async-done(((bf16[1024,1280]{1,0:T(8,128)(2,1)}), bf16[128,1280]{1,0:T(8,128)(2,1)}) %reduce-scatter.4.cloned.1.call-update) | async-done | bytes 327696
  182.4 1.2 copy.26
  183.5 0.8 convert_element_type.61
  184.4 15.8 %all-to-all-start.1 = ((bf16[64,20,128]{2,1,0:T(8,128)(2,1)}), bf16[64,20,128]{2,1,0:T(8,128)(2,1)}, u32[]{:S(2)}, u32[]{:S(2)}) async-start(bf16[64,20,128]{2,1,0:T(8,128)(2,1)} %convert_element_type.61), calls=%async_computation.1 | async-start | bytes 786432 | tf_op jit(solution)/shard_map/all_to_all | solution.py:63
  200.2 0.0 all-gather.2.cloned.1.call-start
  200.3 0.0 copy-done.2
  200.3 0.1 copy.17
  200.4 23.1 %all-to-all-done.1 = bf16[64,20,128]{2,1,0:T(8,128)(2,1)} async-done(((bf16[64,20,128]{2,1,0:T(8,128)(2,1)}), bf16[64,20,128]{2,1,0:T(8,128)(2,1)}, u32[]{:S(2)}, u32[]{:S(2)}) %all-to-all-start.1) | async-done | bytes 327712 | tf_op jit(solution)/shard_map/all_to_all | solution.py:63
  223.6 1.1 reshape.131
  224.6 4.0 gather_fusion
  228.7 2.4 multiply_convert_fusion.2
  231.1 0.0 all-gather.2.cloned.1.call-update
  231.1 0.2 all-reduce.3.cloned.1.call-start
  231.4 35.5 %all-gather.2.cloned.1.call-done = bf16[512,2,1024]{2,1,0:T(2,128)(2,1)} async-done(((bf16[512,2,128]{2,1,0:T(2,128)(2,1)}), bf16[512,2,1024]{2,1,0:T(2,128)(2,1)}) %all-gather.2.cloned.1.call-update) | async-done | bytes 2097168 | tf_op jit(solution)/shard_map/all_gather | solution.py:42
  266.8 4.1 reshape.160
  270.9 7.8 %scatter_custom_fusion.1 = bf16[1280,1024]{1,0:T(8,128)(2,1)} fusion(s32[1024]{0:T(1024)S(1)} %bitcast.48, bf16[1024,1024]{1,0:T(8,128)(2,1)} %reshape.160, bf16[]{:T(256)} %constant.13.clone.1), kind=kCustom, calls=%fused_computation.19 | custom fusion | bytes 2621952 | tf_op jit(solution)/shard_map/scatter | solution.py:26
  278.7 5.2 reshape.129
  283.9 159.6 %all_to_all.16 = bf16[64,20,1024]{2,1,0:T(8,128)(2,1)S(1)} all-to-all(bf16[64,20,1024]{2,1,0:T(8,128)(2,1)} %reshape.129), channel_id=1, replica_groups=mesh['dp'=8,'expert'=64] {'expert'}, dimensions={0} | all-to-all | bytes 5242880 | tf_op jit(solution)/shard_map/all_to_all | solution.py:48
  443.5 2.9 bitcast_convert_fusion
  446.4 0.0 copy-start.3
  446.4 1.0 copy-done.3
  447.3 2.6 convolution_convert_fusion.2
  449.9 0.0 all-reduce.3.cloned.1.call-update
  450.0 0.3 all-reduce.5.cloned.1.call-start
  450.2 73.4 %all-reduce.3.cloned.1.call-done = bf16[1024,1024]{1,0:T(8,128)(2,1)} async-done(((bf16[1024,1024]{1,0:T(8,128)(2,1)}), bf16[1024,1024]{1,0:T(8,128)(2,1)}) %all-reduce.3.cloned.1.call-update) | async-done | bytes 2097168 | tf_op jit(solution)/shard_map/psum | solution.py:21
  523.6 0.0 copy-start.1
  523.6 3.4 fusion
  527.8 0.0 copy-done.1
  527.8 2.9 subtract_convert_fusion
  530.8 0.0 copy-start.4
  530.8 1.0 copy-done.4
  531.7 2.6 convolution_convert_fusion.1
  534.3 0.0 copy-start.5
  534.3 0.0 all-reduce.5.cloned.1.call-update
  534.4 80.9 %all-reduce.5.cloned.1.call-done = bf16[1024,1024]{1,0:T(8,128)(2,1)} async-done(((bf16[1024,1024]{1,0:T(8,128)(2,1)}), bf16[1024,1024]{1,0:T(8,128)(2,1)}) %all-reduce.5.cloned.1.call-update) | async-done | bytes 2097168 | tf_op jit(solution)/shard_map/psum | solution.py:21
  615.2 0.0 copy-done.5
  615.2 4.2 multiply_bitcast_fusion
  (7 shorter events, 0.1 us)
Async XLA Ops:
  7.2 131.1 %copy-start = (bf16[1,1024,512]{2,1,0:T(8,128)(2,1)S(1)}, bf16[1,1024,512]{2,1,0:T(8,128)(2,1)}, u32[]{:S(2)}) copy-start(bf16[1,1024,512]{2,1,0:T(8,128)(2,1)} %param.9) | copy-start | bytes 3145732
  7.2 175.2 %reduce-scatter.4.cloned.1.call-start = ((), (), s32[]{:S(2)}) async-start(), calls=%async_computation.7 | async-start | bytes 2949120
  147.1 53.2 %copy-start.2 = (f32[512,2]{0,1:T(2,128)S(1)}, f32[512,2]{0,1:T(2,128)}, u32[]{:S(2)}) copy-start(f32[512,2]{0,1:T(2,128)} %param.7) | copy-start | bytes 12292
  184.4 39.2 %all-to-all-start.1 = ((bf16[64,20,128]{2,1,0:T(8,128)(2,1)}), bf16[64,20,128]{2,1,0:T(8,128)(2,1)}, u32[]{:S(2)}, u32[]{:S(2)}) async-start(bf16[64,20,128]{2,1,0:T(8,128)(2,1)} %convert_element_type.61), calls=%async_computation.1 | async-start | bytes 786432 | tf_op jit(solution)/shard_map/all_to_all | solution.py:63
  200.2 66.6 %all-gather.2.cloned.1.call-start = ((), (), s32[]{:S(2)}) async-start(), calls=%async_computation.4 | async-start | bytes 2359296 | tf_op jit(solution)/shard_map/all_gather | solution.py:42
  231.1 292.5 %all-reduce.3.cloned.1.call-start = ((), (), s32[]{:S(2)}) async-start(), calls=%async_computation.5 | async-start | bytes 4194304 | tf_op jit(solution)/shard_map/psum | solution.py:21
  446.4 1.0 copy-start.3
  450.0 165.3 %all-reduce.5.cloned.1.call-start = ((), (), s32[]{:S(2)}) async-start(), calls=%async_computation.6 | async-start | bytes 4194304 | tf_op jit(solution)/shard_map/psum | solution.py:21
  523.6 4.2 copy-start.1
  530.8 1.0 copy-start.4
  534.3 80.9 %copy-start.5 = (bf16[1024,512]{1,0:T(8,128)(2,1)S(1)}, bf16[1024,512]{1,0:T(8,128)(2,1)}, u32[]{:S(2)}) copy-start(bf16[1024,512]{1,0:T(8,128)(2,1)} %copy-done.4) | copy-start | bytes 3145732
Sparse Core Ops, SparseCore 0:
  147.2 35.1 reduce-scatter.3
  231.2 35.5 all-gather.1
  450.1 73.4 all-reduce.2
  534.5 80.7 all-reduce.4
where the time goes:
time: 627 us; the launch traced here: 626 us
  blocking collectives  254 us (41%)
  waiting for transfers between devices  248 us (40%)
  local copies, waits for them, and re-layouts  47.8 us (8%)
  other arithmetic  24.9 us (4%)
  matrix products  19.6 us (3%)
  starting transfers between devices  16.4 us (3%)
  between operations  14.7 us (2%)
    all_to_all x1, blocking collectives, per_device(): lax.all_to_all(send_scaled, 'expert', split_axis=0, concat_axis=0, tiled=...  160 us
    psum x2, waiting for transfers between devices, gram_sum(): return lax.psum(partial_gram.astype(jnp.bfloat16), 'dp').astype(jnp.float32)  154 us
    all_to_all x1, blocking collectives, per_device(): lax.all_to_all(send_grad, 'expert', split_axis=0, concat_axis=0, tiled=True)  94.8 us
    all_gather x1, waiting for transfers between devices, per_device(): whole_scaled = lax.all_gather(scaled_part, 'dp', axis=2, tiled=True)  35.5 us
    unnamed x5, waiting for transfers between devices  35.4 us
    all_to_all x1, waiting for transfers between devices, per_device(): lax.all_to_all(summed.reshape(experts, capacity, -1).astype(jnp.bfloat16)...  23.1 us
    scatter x2, local copies, waits for them, and re-layouts, place_slots(): return empty_rows.at[slot_index].set(values)  20.6 us
    another operation x3, other arithmetic  18.2 us
  transfers between devices with their start and end apart: 5, of which 5 were waited for; matrix products, arithmetic and copies ran while one was open for 0% of the time, Pallas kernels for 0%

commit v1 on v0

--- a/solution.py
+++ b/solution.py
@@ -39,7 +39,16 @@
         experts, capacity, width_part
     )
     scaled_part = (gate_prob[:, :, None] * hidden.astype(jnp.float32)).astype(jnp.bfloat16)
-    whole_scaled = lax.all_gather(scaled_part, "dp", axis=2, tiled=True)
+    ways = lax.axis_size("dp")
+    up = [(d, (d + 1) % ways) for d in range(ways)]
+    down = [(d, (d - 1) % ways) for d in range(ways)]
+    earlier, later = ([scaled_part], [scaled_part])
+    for _ in range(ways // 2):
+        earlier.append(lax.ppermute(earlier[-1], "dp", up))
+    for _ in range((ways - 1) // 2):
+        later.append(lax.ppermute(later[-1], "dp", down))
+    line = jnp.concatenate([*earlier[::-1], *later[1:]], axis=2)
+    whole_scaled = jnp.roll(line, (lax.axis_index("dp") - ways // 2) * scaled_part.shape[2], axis=2)
     send_scaled = place_slots(
         slot_index, whole_scaled.reshape(pair_count, -1), total_slots
     ).reshape(experts, capacity, -1)

time: 627 us -> 607 us (0.968)
  blocking collectives: 254 us -> 238 us
  waiting for transfers between devices: 248 us -> 236 us
  starting transfers between devices: 16.4 us -> 24.9 us
    all_gather x1 -> x0, waiting for transfers between devices: 35.5 us -> none  [per_device(): whole_scaled = lax.all_gather(scaled_part, 'dp', axis=2, tiled=True)]
    ppermute x0 -> x7, waiting for transfers between devices: none -> 19.2 us  [the longest x4 19.1 us: per_device(): earlier.append(lax.ppermute(earlier[-1], 'dp', up))]
    all_to_all x1, blocking collectives: 160 us -> 144 us  [per_device(): lax.all_to_all(send_scaled, 'expert', split_axis=0, concat_axis=0, tiled=...]
    ppermute x0 -> x7, starting transfers between devices: none -> 8.87 us  [the longest x3 8.86 us: per_device(): later.append(lax.ppermute(later[-1], 'dp', down))]
    unnamed x5 -> x4, waiting for transfers between devices: 35.4 us -> 35.3 us
  transfers between devices with their start and end apart: 5 -> 11, of which waited for: 5 -> 8; matrix products, arithmetic and copies ran while one was open for 0% -> 0% of each run, Pallas kernels for 0% -> 0%
where the time goes in v1:
time: 607 us; the launch traced here: 606 us
  blocking collectives  238 us (39%)
  waiting for transfers between devices  236 us (39%)
  local copies, waits for them, and re-layouts  48.9 us (8%)
  starting transfers between devices  24.9 us (4%)
  other arithmetic  23.7 us (4%)
  matrix products  19.7 us (3%)
  between operations  14.8 us (2%)
    psum x2, waiting for transfers between devices, gram_sum(): return lax.psum(partial_gram.astype(jnp.bfloat16), 'dp').astype(jnp.float32)  158 us
    all_to_all x1, blocking collectives, per_device(): lax.all_to_all(send_scaled, 'expert', split_axis=0, concat_axis=0, tiled=...  144 us
    all_to_all x1, blocking collectives, per_device(): lax.all_to_all(send_grad, 'expert', split_axis=0, concat_axis=0, tiled=True)  94.8 us
    unnamed x4, waiting for transfers between devices  35.3 us
    all_to_all x1, waiting for transfers between devices, per_device(): lax.all_to_all(summed.reshape(experts, capacity, -1).astype(jnp.bfloat16)...  23 us
    scatter x2, local copies, waits for them, and re-layouts, place_slots(): return empty_rows.at[slot_index].set(values)  20.6 us
    ppermute x4, waiting for transfers between devices, per_device(): earlier.append(lax.ppermute(earlier[-1], 'dp', up))  19.1 us
    another operation x3, other arithmetic  18.2 us
  transfers between devices with their start and end apart: 11, of which 8 were waited for; matrix products, arithmetic and copies ran while one was open for 0% of the time, Pallas kernels for 0%

profile of v1, /device:TPU:2, one launch (start us, length us, event | category | flops | bytes accessed | tf_op | source)
XLA Modules:
  0.0 605.9 jit_solution(9371594036187732509)
XLA Ops:
  7.2 0.8 broadcast_multiply_fusion
  8.0 0.8 copy.19
  8.8 0.2 eq.32
  9.0 0.2 eq.28
  9.2 0.1 copy.18
  9.3 0.2 mul.67
  9.5 18.0 %reduce-window.6 = s32[64,8,128]{2,1,0:T(8,128)S(1)} reduce-window(s32[64,8,128]{2,1,0:T(8,128)S(1)} %fusion.21, s32[]{:T(128)} %constant.56.clone.1), window={size=1x1x128 pad=0_0x0_0x127_0}, to_apply=%region_0.0 | reduce-window | flops 8323072 | bytes 524292 | tf_op jit(solution)/shard_map/reduce-window
  27.6 0.1 slice.12
  27.7 0.1 copy.21
  27.9 0.1 copy.22
  28.0 0.1 broadcast_add_fusion
  28.1 0.1 fusion.20
  28.2 12.8 %scatter_custom_fusion = bf16[1280,512]{1,0:T(8,128)(2,1)S(1)} fusion(s32[1024]{0:T(1024)S(1)} %bitcast.44, bf16[512,512]{1,0:T(8,128)(2,1)} %param.5, s32[1024]{0:T(1024)S(1)} %broadcast_clamp_fusion.1, bf16[]{:T(256)} %constant.54.clone.1), kind=kCustom, calls=%fused_computation.22 | custom fusion | bytes 1311232 | tf_op jit(solution)/shard_map/scatter | solution.py:26
  41.0 1.3 reshape.124
  42.3 94.8 %all_to_all.15 = bf16[64,20,512]{2,1,0:T(8,128)(2,1)S(1)} all-to-all(bf16[64,20,512]{2,1,0:T(8,128)(2,1)} %reshape.124), channel_id=1, replica_groups=mesh['dp'=8,'expert'=64] {'expert'}, dimensions={0} | all-to-all | bytes 2621440 | tf_op jit(solution)/shard_map/all_to_all | solution.py:56
  137.1 1.4 reshape.125
  138.4 4.4 convolution_convert_fusion
  142.8 4.4 copy.25
  147.3 35.3 %reduce-scatter.4.cloned.1.call-done = bf16[128,1280]{1,0:T(8,128)(2,1)} async-done(((bf16[1024,1280]{1,0:T(8,128)(2,1)}), bf16[128,1280]{1,0:T(8,128)(2,1)}) %reduce-scatter.4.cloned.1.call-update) | async-done | bytes 327696
  182.5 1.2 copy.26
  183.7 0.8 convert_element_type.61
  184.5 15.7 %all-to-all-start.1 = ((bf16[64,20,128]{2,1,0:T(8,128)(2,1)}), bf16[64,20,128]{2,1,0:T(8,128)(2,1)S(1)}, u32[]{:S(2)}, u32[]{:S(2)}) async-start(bf16[64,20,128]{2,1,0:T(8,128)(2,1)} %convert_element_type.61), calls=%async_computation.1 | async-start | bytes 786432 | tf_op jit(solution)/shard_map/all_to_all | solution.py:72
  200.2 0.2 all-reduce.3.cloned.1.call-start
  200.5 0.1 copy.17
  200.6 23.0 %all-to-all-done.1 = bf16[64,20,128]{2,1,0:T(8,128)(2,1)S(1)} async-done(((bf16[64,20,128]{2,1,0:T(8,128)(2,1)}), bf16[64,20,128]{2,1,0:T(8,128)(2,1)S(1)}, u32[]{:S(2)}, u32[]{:S(2)}) %all-to-all-start.1) | async-done | bytes 327712 | tf_op jit(solution)/shard_map/all_to_all | solution.py:72
  223.7 0.1 reshape.131
  223.8 2.8 gather_fusion
  226.6 1.4 multiply_convert_fusion.2
  228.0 7.0 %collective-permute-done = bf16[512,2,128]{2,1,0:T(2,128)(2,1)S(1)} collective-permute-done((bf16[512,2,128]{2,1,0:T(2,128)(2,1)S(1)}, bf16[512,2,128]{2,1,0:T(2,128)(2,1)S(1)}, u32[]{:S(2)}, u32[]{:S(2)}) %collective-permute-start) | collective-permute-done | bytes 262176 | tf_op jit(solution)/shard_map/ppermute | solution.py:47
  235.0 3.0 collective-permute-start.4
  237.9 4.1 collective-permute-done.1
  242.0 3.0 collective-permute-start.5
  244.9 4.0 collective-permute-done.2
  249.0 3.0 collective-permute-start.6
  251.9 4.0 collective-permute-done.3
  256.0 0.2 constant_dynamic-update-slice_fusion.15
  256.2 0.4 constant_dynamic-update-slice_fusion.14
  256.5 0.4 constant_dynamic-update-slice_fusion.13
  256.9 0.4 constant_dynamic-update-slice_fusion.12
  257.3 0.4 constant_dynamic-update-slice_fusion.11
  257.6 0.4 constant_dynamic-update-slice_fusion.10
  258.0 0.4 constant_dynamic-update-slice_fusion.9
  258.4 0.4 constant_dynamic-update-slice_fusion.8
  258.8 0.4 constant_dynamic-update-slice_fusion.7
  259.1 0.4 constant_dynamic-update-slice_fusion.6
  259.5 0.4 constant_dynamic-update-slice_fusion.5
  259.9 0.4 constant_dynamic-update-slice_fusion.4
  260.2 0.4 constant_dynamic-update-slice_fusion.3
  260.6 0.4 constant_dynamic-update-slice_fusion.2
  261.0 0.4 constant_dynamic-update-slice_fusion.1
  261.4 0.4 constant_dynamic-update-slice_fusion
  261.7 1.4 constant_dynamic-slice_fusion
  263.2 2.2 reshape.160
  265.4 7.8 %scatter_custom_fusion.1 = bf16[1280,1024]{1,0:T(8,128)(2,1)} fusion(s32[1024]{0:T(1024)S(1)} %bitcast.46, bf16[1024,1024]{1,0:T(8,128)(2,1)} %reshape.160, bf16[]{:T(256)} %constant.54.clone.1), kind=kCustom, calls=%fused_computation.19 | custom fusion | bytes 2621952 | tf_op jit(solution)/shard_map/scatter | solution.py:26
  273.2 5.2 reshape.129
  278.4 143.6 %all_to_all.16 = bf16[64,20,1024]{2,1,0:T(8,128)(2,1)S(1)} all-to-all(bf16[64,20,1024]{2,1,0:T(8,128)(2,1)} %reshape.129), channel_id=1, replica_groups=mesh['dp'=8,'expert'=64] {'expert'}, dimensions={0} | all-to-all | bytes 5242880 | tf_op jit(solution)/shard_map/all_to_all | solution.py:57
  422.0 2.9 bitcast_convert_fusion
  424.9 2.6 convolution_convert_fusion.2
  427.5 77.1 %all-reduce.3.cloned.1.call-done = bf16[1024,1024]{1,0:T(8,128)(2,1)} async-done(((bf16[1024,1024]{1,0:T(8,128)(2,1)}), bf16[1024,1024]{1,0:T(8,128)(2,1)}) %all-reduce.3.cloned.1.call-update) | async-done | bytes 2097168 | tf_op jit(solution)/shard_map/psum | solution.py:21
  504.6 3.3 fusion
  508.7 3.0 subtract_convert_fusion
  511.6 2.6 convolution_convert_fusion.1
  514.3 80.9 %all-reduce.5.cloned.1.call-done = bf16[1024,1024]{1,0:T(8,128)(2,1)} async-done(((bf16[1024,1024]{1,0:T(8,128)(2,1)}), bf16[1024,1024]{1,0:T(8,128)(2,1)}) %all-reduce.5.cloned.1.call-update) | async-done | bytes 2097168 | tf_op jit(solution)/shard_map/psum | solution.py:21
  595.2 4.2 multiply_bitcast_fusion
  (29 shorter events, 0.3 us)
Async XLA Ops:
  7.2 131.3 %copy-start = (bf16[1,1024,512]{2,1,0:T(8,128)(2,1)S(1)}, bf16[1,1024,512]{2,1,0:T(8,128)(2,1)}, u32[]{:S(2)}) copy-start(bf16[1,1024,512]{2,1,0:T(8,128)(2,1)} %param.9) | copy-start | bytes 3145732
  7.2 175.4 %reduce-scatter.4.cloned.1.call-start = ((), (), s32[]{:S(2)}) async-start(), calls=%async_computation.6 | async-start | bytes 2949120
  137.1 5.8 copy-start.1
  147.2 53.2 %copy-start.4 = (f32[512,2]{0,1:T(2,128)S(1)}, f32[512,2]{0,1:T(2,128)}, u32[]{:S(2)}) copy-start(f32[512,2]{0,1:T(2,128)} %param.7) | copy-start | bytes 12292
  184.5 39.1 %all-to-all-start.1 = ((bf16[64,20,128]{2,1,0:T(8,128)(2,1)}), bf16[64,20,128]{2,1,0:T(8,128)(2,1)S(1)}, u32[]{:S(2)}, u32[]{:S(2)}) async-start(bf16[64,20,128]{2,1,0:T(8,128)(2,1)} %convert_element_type.61), calls=%async_computation.1 | async-start | bytes 786432 | tf_op jit(solution)/shard_map/all_to_all | solution.py:72
  200.2 304.4 %all-reduce.3.cloned.1.call-start = ((), (), s32[]{:S(2)}) async-start(), calls=%async_computation.4 | async-start | bytes 4194304 | tf_op jit(solution)/shard_map/psum | solution.py:21
  223.8 2.8 copy-start.3
  228.0 7.0 %collective-permute-start = (bf16[512,2,128]{2,1,0:T(2,128)(2,1)S(1)}, bf16[512,2,128]{2,1,0:T(2,128)(2,1)S(1)}, u32[]{:S(2)}, u32[]{:S(2)}) collective-permute-start(bf16[512,2,128]{2,1,0:T(2,128)(2,1)S(1)} %get-tuple-element.2), channel_id=1, source_target_pairs={{0,64},{64,128},{128,192},{192,256},{256,320},{320,384},{384,448},... | collective-permute-start | bytes 786440 | tf_op jit(solution)/shard_map/ppermute | solution.py:47
  235.0 7.0 %collective-permute-start.1 = (bf16[512,2,128]{2,1,0:T(2,128)(2,1)S(1)}, bf16[512,2,128]{2,1,0:T(2,128)(2,1)S(1)}, u32[]{:S(2)}, u32[]{:S(2)}) collective-permute-start(bf16[512,2,128]{2,1,0:T(2,128)(2,1)S(1)} %collective-permute-done), channel_id=1, source_target_pairs={{0,64},{64,128},{128,192},{192,256},{256,320},{320,384},{384,448},... | collective-permute-start | bytes 786440 | tf_op jit(solution)/shard_map/ppermute | solution.py:47
  235.0 7.0 %collective-permute-start.4 = (bf16[512,2,128]{2,1,0:T(2,128)(2,1)S(1)}, bf16[512,2,128]{2,1,0:T(2,128)(2,1)S(1)}, u32[]{:S(2)}, u32[]{:S(2)}) collective-permute-start(bf16[512,2,128]{2,1,0:T(2,128)(2,1)S(1)} %get-tuple-element.2), channel_id=1, source_target_pairs={{0,448},{64,0},{128,64},{192,128},{256,192},{320,256},{384,320},{4... | collective-permute-start | bytes 786440 | tf_op jit(solution)/shard_map/ppermute | solution.py:49
  242.0 7.0 %collective-permute-start.2 = (bf16[512,2,128]{2,1,0:T(2,128)(2,1)S(1)}, bf16[512,2,128]{2,1,0:T(2,128)(2,1)S(1)}, u32[]{:S(2)}, u32[]{:S(2)}) collective-permute-start(bf16[512,2,128]{2,1,0:T(2,128)(2,1)S(1)} %collective-permute-done.1), channel_id=1, source_target_pairs={{0,64},{64,128},{128,192},{192,256},{256,320},{320,384},{384,448},... | collective-permute-start | bytes 786440 | tf_op jit(solution)/shard_map/ppermute | solution.py:47
  242.0 7.0 %collective-permute-start.5 = (bf16[512,2,128]{2,1,0:T(2,128)(2,1)S(1)}, bf16[512,2,128]{2,1,0:T(2,128)(2,1)S(1)}, u32[]{:S(2)}, u32[]{:S(2)}) collective-permute-start(bf16[512,2,128]{2,1,0:T(2,128)(2,1)S(1)} %collective-permute-done.4), channel_id=1, source_target_pairs={{0,448},{64,0},{128,64},{192,128},{256,192},{320,256},{384,320},{4... | collective-permute-start | bytes 786440 | tf_op jit(solution)/shard_map/ppermute | solution.py:49
  249.0 7.0 %collective-permute-start.3 = (bf16[512,2,128]{2,1,0:T(2,128)(2,1)S(1)}, bf16[512,2,128]{2,1,0:T(2,128)(2,1)S(1)}, u32[]{:S(2)}, u32[]{:S(2)}) collective-permute-start(bf16[512,2,128]{2,1,0:T(2,128)(2,1)S(1)} %collective-permute-done.2), channel_id=1, source_target_pairs={{0,64},{64,128},{128,192},{192,256},{256,320},{320,384},{384,448},... | collective-permute-start | bytes 786440 | tf_op jit(solution)/shard_map/ppermute | solution.py:47
  249.0 9.4 %collective-permute-start.6 = (bf16[512,2,128]{2,1,0:T(2,128)(2,1)S(1)}, bf16[512,2,128]{2,1,0:T(2,128)(2,1)S(1)}, u32[]{:S(2)}, u32[]{:S(2)}) collective-permute-start(bf16[512,2,128]{2,1,0:T(2,128)(2,1)S(1)} %collective-permute-done.5), channel_id=1, source_target_pairs={{0,448},{64,0},{128,64},{192,128},{256,192},{320,256},{384,320},{4... | collective-permute-start | bytes 786440 | tf_op jit(solution)/shard_map/ppermute | solution.py:49
  278.4 143.6 %copy-start.2 = (bf16[64,20,512]{2,1,0:T(8,128)(2,1)S(1)}, bf16[64,20,512]{2,1,0:T(8,128)(2,1)}, u32[]{:S(2)}) copy-start(bf16[64,20,512]{2,1,0:T(8,128)(2,1)} %copy-done.1) | copy-start | bytes 3932164
  427.5 167.7 %all-reduce.5.cloned.1.call-start = ((), (), s32[]{:S(2)}) async-start(), calls=%async_computation.5 | async-start | bytes 4194304 | tf_op jit(solution)/shard_map/psum | solution.py:21
Sparse Core Ops, SparseCore 0:
  147.4 35.1 reduce-scatter.3
  427.6 76.9 all-reduce.2
  514.4 80.7 all-reduce.4
